TPU v7x, 32 devices: a whole 2x2x4 slice. The times are simulated.
32 devices in a mesh: req: 8 (over z, x), cfg: 2 (over core), seq: 2 (over y).
Axes of the slice: x: 2, y: 2, z: 4, core: 2. Of those that a mesh axis runs over, the one named last changes fastest.
Arguments:
- queries: bfloat16 [8, 2, 512, 1024], P('req', 'cfg', 'seq'), may hold values from -48 to 48
- key_vectors: bfloat16 [8, 2, 512, 1024], P('req', 'cfg', 'seq'), may hold values from -48 to 48
- values: bfloat16 [8, 2, 512, 1024], P('req', 'cfg', 'seq'), may hold values from -6 to 6
- hidden: bfloat16 [8, 2, 512, 1536], P('req', 'cfg', 'seq'), may hold values from -15 to 15
- out_proj: bfloat16 [1024, 1536], P('req'), may hold values from -0.1875 to 0.1875
- head_weight: bfloat16 [1536, 64], replicated, may hold values from -0.15625 to 0.15625
- head_bias: float32 [64], replicated, may hold values from -3 to 3
- attn_gate: float32 [8, 1536], P('req'), may hold values from 0.5 to 4
- shift_scale: float32 [8, 2, 1536], P('req'), may hold values from -3 to 3
- grid_shape: int32 [8, 3], P('req'), may hold values from 1 to 32, as said below
- step_index: int32 [8], P('req'), may hold values from 0 to 19
- guide_scale: float32 [8], P('req'), may hold values from 3 to 6
- latent: float32 [8, 512, 64], P('req', 'seq', 'cfg'), may hold values from -6 to 6
Outputs:
- next_latent: float32 [8, 512, 64], P('req', 'seq', 'cfg')
- velocity: float32 [8, 512, 64], P('req', 'seq', 'cfg')
Inputs may be any that keep to these rules, and one draw needn't show every extreme that they name: `grid_shape`: the frames are at most 2, the height at most 8 and the width at most 32, so that frames * height * width is at most 512; in every draw some request fills all 512 slots.
All inputs are finite; a program needn't handle non-finite values.
Results may differ from a plain program's by a relative error of at most 0.0052.
Values may be sent and summed in bfloat16 or wider, within the bound.
A program may use at most 64 MiB of HBM per device.

v0:
```python
import math

import jax
import jax.numpy as jnp
from jax import lax
from jax.sharding import PartitionSpec as P

HEAD_DIM = 128
STEPS = 20


masked_score = -1e30
norm_eps = 1e-06
shift_factor = 5.0


def partner_2(block, axis, distance):
    count = lax.axis_size(axis)
    route = []
    for low in range(count):
        high = low | 1 << distance
        if high != low and high < count:
            route += [(low, high), (high, low)]
    return lax.ppermute(block, axis, route)


def rotary(vectors, grid_dims, first_token):
    row_count, col_count = vectors.shape
    sixth_dim = HEAD_DIM // 6
    time_pairs = (HEAD_DIM - 4 * sixth_dim) // 2
    column = jnp.arange(col_count, dtype=jnp.int32) % HEAD_DIM
    pair_index = column // 2
    space_pair = (pair_index - time_pairs).astype(jnp.float32)
    is_time = pair_index < time_pairs
    is_height = jnp.logical_and(pair_index >= time_pairs, pair_index < time_pairs + sixth_dim)
    exponent = jnp.where(
        is_time,
        pair_index.astype(jnp.float32) / time_pairs,
        jnp.where(is_height, space_pair / sixth_dim, (space_pair - sixth_dim) / sixth_dim),
    )
    frequency = jnp.power(jnp.float32(10000.0), -exponent)
    token_ids = first_token + jnp.arange(row_count, dtype=jnp.int32)
    plane_size = grid_dims[1] * grid_dims[2]
    frame_ids = token_ids // plane_size
    height = token_ids // grid_dims[2] % grid_dims[1]
    across = token_ids % grid_dims[2]
    position = jnp.where(
        is_time[None, :],
        frame_ids[:, None],
        jnp.where(is_height[None, :], height[:, None], across[:, None]),
    ).astype(jnp.float32)
    angles = position * frequency[None, :]
    is_even = column % 2 == 0
    source = vectors.astype(jnp.float32)
    partner = jnp.where(is_even[None, :], jnp.roll(source, -1, axis=1), jnp.roll(source, 1, axis=1))
    sign_flip = jnp.where(is_even, -1.0, 1.0).astype(jnp.float32)
    turned = source * jnp.cos(angles) + partner * (jnp.sin(angles) * sign_flip[None, :])
    return turned.astype(jnp.bfloat16)


def noise_level(step_value):
    progress = 1.0 - step_value.astype(jnp.float32) / STEPS
    return shift_factor * progress / (1.0 + (shift_factor - 1.0) * progress)


def output_head(hidden_rows, proj, gate_row, modulation, head_weight, head_bias):
    mixed_rows = hidden_rows.astype(jnp.float32) + gate_row[None, :] * proj
    average = jnp.mean(mixed_rows, axis=-1, keepdims=True)
    centered = mixed_rows - average
    spread = jnp.mean(centered * centered, axis=-1, keepdims=True)
    normed = centered * lax.rsqrt(spread + norm_eps)
    modded = (normed * (1.0 + modulation[1][None, :]) + modulation[0][None, :]).astype(jnp.bfloat16)
    return jnp.dot(modded, head_weight, preferred_element_type=jnp.float32) + head_bias[None, :]


def attend_all(query_heads, key_heads, value_heads, length):
    total_rows = query_heads.shape[0]
    block_rows = min(512, total_rows)
    score_scale = 1.0 / math.sqrt(HEAD_DIM)
    live_keys = jnp.arange(total_rows, dtype=jnp.int32) < length

    def one_block(start):
        query_block = lax.dynamic_slice_in_dim(query_heads, start, block_rows, 0)
        scores = (
            jnp.einsum("qhd,khd->hqk", query_block, key_heads, preferred_element_type=jnp.float32)
            * score_scale
        )
        scores = jnp.where(live_keys[None, None, :], scores, masked_score)
        row_max = jnp.max(scores, axis=-1, keepdims=True)
        exponent = jnp.exp(scores - row_max)
        row_sum = jnp.sum(exponent, axis=-1, keepdims=True)
        weights = (exponent / row_sum).astype(jnp.bfloat16)
        output = jnp.einsum(
            "hqk,khd->qhd", weights, value_heads, preferred_element_type=jnp.float32
        )
        return output.astype(jnp.bfloat16)

    starts = jnp.arange(total_rows // block_rows, dtype=jnp.int32) * block_rows
    return lax.map(one_block, starts).reshape(total_rows, -1)


def on_device(
    queries,
    key_vectors,
    values,
    hidden,
    out_proj,
    head_weight,
    head_bias,
    attn_gate,
    shift_scale,
    grid_shape,
    step_index,
    guide_scale,
    latent,
):
    row_count = queries.shape[2]
    grid_dims = grid_shape[0]
    length = grid_dims[0] * grid_dims[1] * grid_dims[2]
    first_token = lax.axis_index("seq") * row_count
    rot_q = rotary(queries[0, 0], grid_dims, first_token)
    rot_k = rotary(key_vectors[0, 0], grid_dims, first_token)
    head_q, head_k, head_v = (
        lax.all_to_all(rot_q, "seq", split_axis=1, concat_axis=0, tiled=True),
        lax.all_to_all(rot_k, "seq", split_axis=1, concat_axis=0, tiled=True),
        lax.all_to_all(values[0, 0], "seq", split_axis=1, concat_axis=0, tiled=True),
    )
    total_rows = head_q.shape[0]
    local_heads = head_q.shape[1] // HEAD_DIM
    head_shape = (total_rows, local_heads, HEAD_DIM)
    query_heads = head_q.reshape(head_shape)
    key_heads = head_k.reshape(head_shape)
    value_heads = head_v.reshape(head_shape)
    head_result = attend_all(query_heads, key_heads, value_heads, length)
    attended = lax.all_to_all(head_result, "seq", split_axis=0, concat_axis=1, tiled=True)
    proj = jnp.dot(
        attended,
        lax.all_gather(out_proj, "req", axis=0, tiled=True),
        preferred_element_type=jnp.float32,
    )
    prediction = output_head(
        hidden[0, 0], proj, attn_gate[0], shift_scale[0], head_weight, head_bias
    )
    own_width = latent.shape[2]
    cfg_place = lax.axis_index("cfg")
    own_cols = lax.dynamic_slice_in_dim(prediction, cfg_place * own_width, own_width, 1)
    partner_cols = lax.dynamic_slice_in_dim(prediction, (1 - cfg_place) * own_width, own_width, 1)
    other_half = partner_2(partner_cols, "cfg", 0)
    is_cond = cfg_place == 0
    cond_pred = jnp.where(is_cond, own_cols, other_half)
    uncond_pred = jnp.where(is_cond, other_half, own_cols)
    guided = uncond_pred + guide_scale[0] * (cond_pred - uncond_pred)
    live_rows = first_token + jnp.arange(row_count, dtype=jnp.int32) < length
    velocity = jnp.where(live_rows[:, None], guided, jnp.float32(0.0))
    delta_level = noise_level(step_index[0] + 1) - noise_level(step_index[0])
    next_latent = latent[0] + delta_level * velocity
    return (next_latent[None], velocity[None])


def solution(mesh):
    return jax.shard_map(
        on_device,
        mesh=mesh,
        in_specs=(
            P("req", "cfg", "seq", None),
            P("req", "cfg", "seq", None),
            P("req", "cfg", "seq", None),
            P("req", "cfg", "seq", None),
            P("req", None),
            P(),
            P(),
            P("req", None),
            P("req", None, None),
            P("req", None),
            P("req"),
            P("req"),
            P("req", "seq", "cfg"),
        ),
        out_specs=(P("req", "seq", "cfg"), P("req", "seq", "cfg")),
        check_vma=False,
    )
```

profile of v0, /device:TPU:0, one launch (start us, length us, event | category | flops | bytes accessed | tf_op | source)
XLA Modules:
  0.0 87.9 jit_solution(608926784474118634)
XLA Ops:
  7.2 0.7 all-gather.2.cloned.1.call-update
  7.9 1.4 %fusion.34 = (s32[1,1]{1,0:T(1,128)}, s32[1,1]{1,0:T(1,128)}, s32[1,1]{1,0:T(1,128)}) fusion(s32[1,3]{1,0:T(1,128)} %param.22), kind=kLoop, calls=%fused_computation.78 | loop fusion | bytes 24 | tf_op jit(solution)/shard_map/slice | solution.py:119
  14.0 2.1 %reshape.291 = f32[256,2,512]{2,1,0:T(2,128)S(1)} reshape(bf16[1,1,256,1024]{3,2,1,0:T(8,128)(2,1)} %param.13) | data formatting | bytes 1572864 | tf_op jit(solution)/shard_map/convert_element_type | solution.py:54
  16.1 2.1 %reshape.293 = f32[256,2,512]{2,1,0:T(2,128)S(1)} reshape(bf16[1,1,256,1024]{3,2,1,0:T(8,128)(2,1)} %param.14) | data formatting | bytes 1572864 | tf_op jit(solution)/shard_map/convert_element_type | solution.py:54
  18.1 0.1 and_select_fusion.6
  18.3 0.9 %and_select_fusion.3 = (s32[256]{0:T(256)S(1)}, s32[256]{0:T(256)S(1)}) fusion(pred[]{:T(512)S(6)} %lt.119, s32[]{:T(128)S(6)} %select_n.201, s32[]{:T(128)S(6)} %mul.133, pred[]{:T(512)S(6)} %lt.117, s32[]{:T(128)S(6)} %select_n.199, s32[]{:T(128)} %bitcast.4, s32[]{:T(128)S(6)} %sign.48), kind=kLoop, calls=%fused_computation.61 | loop fusion | flops 5888 | bytes 2070 | tf_op jit(solution)/shard_map/jit(remainder)/select_n | solution.py:46
  19.5 0.4 fusion.32
  19.9 0.4 pad_maximum_fusion.2
  20.4 0.6 copy-done.2
  21.2 0.4 fusion.30
  21.6 0.4 pad_maximum_fusion
  22.1 5.4 %fusion.14 = (bf16[256,2,512]{2,0,1:T(8,128)(2,1)S(1)}, bf16[256,2,512]{2,0,1:T(8,128)(2,1)}) fusion(f32[32,2,8,512]{3,2,1,0:T(8,128)S(1)} %bitcast.64, f32[32,2,8,512]{3,2,1,0:T(8,128)S(1)} %bitcast.63, f32[256,2,512]{2,1,0:T(2,128)S(1)} %reshape.291, f32[2,512]{1,0:T(2,128)S(1)} %get-tuple-element.50, f32[2,512]{1,0:T(2,128)S(1)} %get-tuple-element.49, ...), kind=kLoop, calls=%fused_computation.23 | loop fusion | flops 3932160 | bytes 7354368 | tf_op jit(solution)/shard_map/convert_element_type | solution.py:58
  27.5 12.0 %all_to_all.61 = bf16[256,2,512]{2,0,1:T(8,128)(2,1)S(1)} all-to-all(bf16[256,2,512]{2,0,1:T(8,128)(2,1)S(1)} %get-tuple-element.32), channel_id=1, replica_groups=mesh['req'=8,'cfg'=2,'seq'=2] {'seq'}, dimensions={1} | all-to-all | bytes 1048576 | tf_op jit(solution)/shard_map/all_to_all | solution.py:124
  39.5 3.5 %all-to-all-start.1 = ((bf16[256,2,512]{2,0,1:T(8,128)(2,1)}), bf16[256,2,512]{2,0,1:T(8,128)(2,1)S(1)}, u32[]{:S(2)}, u32[]{:S(2)}) async-start(bf16[256,2,512]{2,0,1:T(8,128)(2,1)} %get-tuple-element.33), calls=%async_computation.1 | async-start | bytes 1048576 | tf_op jit(solution)/shard_map/all_to_all | solution.py:125
  43.0 0.4 all_to_all.50
  43.4 0.9 copy.24
  44.2 5.8 %all-to-all-done.1 = bf16[256,2,512]{2,0,1:T(8,128)(2,1)S(1)} async-done(((bf16[256,2,512]{2,0,1:T(8,128)(2,1)}), bf16[256,2,512]{2,0,1:T(8,128)(2,1)S(1)}, u32[]{:S(2)}, u32[]{:S(2)}) %all-to-all-start.1) | async-done | bytes 524320 | tf_op jit(solution)/shard_map/all_to_all | solution.py:125
  50.0 3.5 %all-to-all-start.2 = ((bf16[256,2,512]{2,0,1:T(8,128)(2,1)}), bf16[256,2,512]{2,0,1:T(8,128)(2,1)S(1)}, u32[]{:S(2)}, u32[]{:S(2)}) async-start(bf16[256,2,512]{2,0,1:T(8,128)(2,1)} %copy.24), calls=%async_computation.2 | async-start | bytes 1048576 | tf_op jit(solution)/shard_map/all_to_all | solution.py:126
  55.5 0.1 reshape.281
  55.8 4.3 %all-to-all-done.2 = bf16[256,2,512]{2,0,1:T(8,128)(2,1)S(1)} async-done(((bf16[256,2,512]{2,0,1:T(8,128)(2,1)}), bf16[256,2,512]{2,0,1:T(8,128)(2,1)S(1)}, u32[]{:S(2)}, u32[]{:S(2)}) %all-to-all-start.2) | async-done | bytes 524320 | tf_op jit(solution)/shard_map/all_to_all | solution.py:126
  60.2 0.7 fusion.20
  60.9 1.4 %fusion.35 = (f32[4,512]{1,0:T(4,128)S(1)}, f32[4,512,512]{1,2,0:T(8,128)S(1)}) fusion(f32[4,512,512]{1,2,0:T(8,128)S(1)} %fusion.20, pred[512]{0:T(512)(128)(4,1)S(1)} %iota_compare_fusion), kind=kOutput, calls=%fused_computation.79 | output fusion | flops 6291967 | bytes 8397312 | tf_op jit(solution)/shard_map/while/body/eval_jaxpr/sub | solution.py:90
  62.3 0.9 %fusion.8 = bf16[512,4,128]{2,0,1:T(8,128)(2,1)S(1)} fusion(f32[4,512,512]{1,2,0:T(8,128)S(1)} %get-tuple-element.38, f32[4,512]{1,0:T(4,128)S(1)} %get-tuple-element.37, bf16[512,4,128]{2,1,0:T(4,128)(2,1)S(1)} %reshape.283), kind=kOutput, calls=%fused_computation.14 | convolution fusion | flops 270794752 | bytes 5251072 | tf_op jit(solution)/shard_map/while/body/eval_jaxpr/hqk,khd->qhd/dot_general | solution.py:93
  63.3 0.4 copy.27
  63.7 1.0 %all_to_all.53 = bf16[2,256,512]{2,1,0:T(8,128)(2,1)} reshape(bf16[512,4,128]{2,1,0:T(4,128)(2,1)S(1)} %copy.27) | data formatting | bytes 1048576 | tf_op jit(solution)/shard_map/all_to_all | solution.py:135
  64.7 3.5 %all-to-all-start.3 = ((bf16[2,256,512]{2,1,0:T(8,128)(2,1)}), bf16[2,256,512]{2,1,0:T(8,128)(2,1)S(1)}, u32[]{:S(2)}, u32[]{:S(2)}) async-start(bf16[2,256,512]{2,1,0:T(8,128)(2,1)} %all_to_all.53), calls=%async_computation.3 | async-start | bytes 1048576 | tf_op jit(solution)/shard_map/all_to_all | solution.py:135
  68.3 6.5 %all-to-all-done.3 = bf16[2,256,512]{2,1,0:T(8,128)(2,1)S(1)} async-done(((bf16[2,256,512]{2,1,0:T(8,128)(2,1)}), bf16[2,256,512]{2,1,0:T(8,128)(2,1)S(1)}, u32[]{:S(2)}, u32[]{:S(2)}) %all-to-all-start.3) | async-done | bytes 524320 | tf_op jit(solution)/shard_map/all_to_all | solution.py:135
  74.8 0.2 copy.28
  75.0 3.0 %fusion.36 = (f32[256]{0:T(256)S(1)}, f32[256,1536]{1,0:T(8,128)S(1)}) fusion(bf16[256,1024]{0,1:T(8,128)(2,1)S(1)} %bitcast.69, bf16[1024,1536]{1,0:T(8,128)(2,1)} %all-gather.2.cloned.1.call-done, f32[1536]{0:T(1024)S(1)} %reduce, bf16[1,1,256,1536]{3,2,1,0:T(8,128)(2,1)S(1)} %copy-done.7), kind=kOutput, calls=%fused_computation.80 | convolution fusion | flops 806878976 | bytes 6036480 | tf_op jit(solution)/shard_map/dot_general | solution.py:136
  78.0 0.3 multiply_reduce_fusion
  78.4 0.5 convolution_add_fusion
  80.4 0.6 fusion.25
  (37 shorter events, 1.0 us)
Async XLA Ops:
  7.2 71.2 %copy-start = (bf16[1536,64]{0,1:T(8,128)(2,1)S(1)}, bf16[1536,64]{0,1:T(8,128)(2,1)}, u32[]{:S(2)}) copy-start(bf16[1536,64]{0,1:T(8,128)(2,1)} %param.18) | copy-start | bytes 589828
  7.2 12.1 %copy-start.1 = (bf16[1,1,256,1024]{3,2,1,0:T(8,128)(2,1)S(1)}, bf16[1,1,256,1024]{3,2,1,0:T(8,128)(2,1)}, u32[]{:S(2)}) copy-start(bf16[1,1,256,1024]{3,2,1,0:T(8,128)(2,1)} %param.14) | copy-start | bytes 1572868
  7.2 67.8 %all-gather.2.cloned.1.call-start = ((), (), s32[]{:S(2)}) async-start(), calls=%async_computation.4 | async-start | bytes 3538944 | tf_op jit(solution)/shard_map/all_gather | solution.py:138
  19.9 1.1 %copy-start.2 = (bf16[1,1,256,1024]{3,2,1,0:T(8,128)(2,1)S(1)}, bf16[1,1,256,1024]{3,2,1,0:T(8,128)(2,1)}, u32[]{:S(2)}) copy-start(bf16[1,1,256,1024]{3,2,1,0:T(8,128)(2,1)} %param.13) | copy-start | bytes 1572868
  22.0 20.9 %copy-start.3 = (bf16[1,1,256,1024]{3,2,1,0:T(8,128)(2,1)S(1)}, bf16[1,1,256,1024]{3,2,1,0:T(8,128)(2,1)}, u32[]{:S(2)}) copy-start(bf16[1,1,256,1024]{3,2,1,0:T(8,128)(2,1)} %param.15) | copy-start | bytes 1572868
  39.5 10.5 %all-to-all-start.1 = ((bf16[256,2,512]{2,0,1:T(8,128)(2,1)}), bf16[256,2,512]{2,0,1:T(8,128)(2,1)S(1)}, u32[]{:S(2)}, u32[]{:S(2)}) async-start(bf16[256,2,512]{2,0,1:T(8,128)(2,1)} %get-tuple-element.33), calls=%async_computation.1 | async-start | bytes 1048576 | tf_op jit(solution)/shard_map/all_to_all | solution.py:125
  50.0 10.1 %all-to-all-start.2 = ((bf16[256,2,512]{2,0,1:T(8,128)(2,1)}), bf16[256,2,512]{2,0,1:T(8,128)(2,1)S(1)}, u32[]{:S(2)}, u32[]{:S(2)}) async-start(bf16[256,2,512]{2,0,1:T(8,128)(2,1)} %copy.24), calls=%async_computation.2 | async-start | bytes 1048576 | tf_op jit(solution)/shard_map/all_to_all | solution.py:126
  63.3 5.0 %copy-start.6 = (f32[1,1536]{1,0:T(1,128)S(1)}, f32[1,1536]{1,0:T(1,128)}, u32[]{:S(2)}) copy-start(f32[1,1536]{1,0:T(1,128)} %param.20) | copy-start | bytes 18436
  63.3 5.0 %copy-start.5 = (f32[1,2,1536]{2,1,0:T(2,128)S(1)}, f32[1,2,1536]{2,1,0:T(2,128)}, u32[]{:S(2)}) copy-start(f32[1,2,1536]{2,1,0:T(2,128)} %param.21) | copy-start | bytes 36868
  63.3 11.7 %copy-start.7 = (bf16[1,1,256,1536]{3,2,1,0:T(8,128)(2,1)S(1)}, bf16[1,1,256,1536]{3,2,1,0:T(8,128)(2,1)}, u32[]{:S(2)}) copy-start(bf16[1,1,256,1536]{3,2,1,0:T(8,128)(2,1)} %param.16) | copy-start | bytes 2359300
  64.7 10.1 %all-to-all-start.3 = ((bf16[2,256,512]{2,1,0:T(8,128)(2,1)}), bf16[2,256,512]{2,1,0:T(8,128)(2,1)S(1)}, u32[]{:S(2)}, u32[]{:S(2)}) async-start(bf16[2,256,512]{2,1,0:T(8,128)(2,1)} %all_to_all.53), calls=%async_computation.3 | async-start | bytes 1048576 | tf_op jit(solution)/shard_map/all_to_all | solution.py:135
  75.0 3.3 %copy-start.8 = (f32[64]{0:T(128)S(1)}, f32[64]{0:T(128)}, u32[]{:S(2)}) copy-start(f32[64]{0:T(128)} %param.19) | copy-start | bytes 772
  78.0 2.4 %copy-start.4 = (f32[1,256,32]{1,2,0:T(8,128)S(1)}, f32[1,256,32]{1,2,0:T(8,128)}, u32[]{:S(2)}) copy-start(f32[1,256,32]{1,2,0:T(8,128)} %param.25) | copy-start | bytes 98308
  78.9 1.5 %collective-permute-start = (f32[256,32]{0,1:T(8,128)S(1)}, f32[256,32]{0,1:T(8,128)S(1)}, u32[]{:S(2)}, u32[]{:S(2)}) collective-permute-start(f32[256,32]{0,1:T(8,128)S(1)} %constant_dynamic-slice_fusion), channel_id=1, source_target_pairs={{0,2},{2,0},{1,3},{3,1},{4,6},{6,4},{5,7},{7,5},{8,10},{10,8},{9,1... | collective-permute-start | bytes 98312 | tf_op jit(solution)/shard_map/ppermute | solution.py:24
Sparse Core Ops, SparseCore 0:
  10.2 63.1 all-gather.1
where the time goes:
time: 88.6 us; the launch traced here: 87.9 us
  between operations  22.4 us (25%)
  waiting for transfers between devices  17.3 us (20%)
  blocking collectives  12 us (14%)
  starting transfers between devices  10.6 us (12%)
  local copies, waits for them, and re-layouts  10.5 us (12%)
  other arithmetic  10.1 us (11%)
  matrix products  5.09 us (6%)
    all_to_all x1, blocking collectives, on_device(): lax.all_to_all(rot_q, 'seq', split_axis=1, concat_axis=0, tiled=True)  12 us
    all_to_all x1, waiting for transfers between devices, on_device(): lax.all_to_all(head_result, 'seq', split_axis=0, concat_axis=1, tiled=True)  6.46 us
    all_to_all x1, waiting for transfers between devices, on_device(): lax.all_to_all(rot_k, 'seq', split_axis=1, concat_axis=0, tiled=True)  5.78 us
    convert_element_type x1, other arithmetic, rotary(): return turned.astype(jnp.bfloat16)  5.45 us
    all_to_all x1, waiting for transfers between devices, on_device(): lax.all_to_all(values[0, 0], 'seq', split_axis=1, concat_axis=0, tiled=True)  4.32 us
    convert_element_type x2, local copies, waits for them, and re-layouts, rotary(): source = vectors.astype(jnp.float32)  4.14 us
    all_to_all x1, starting transfers between devices, on_device(): lax.all_to_all(values[0, 0], 'seq', split_axis=1, concat_axis=0, tiled=True)  3.49 us
    all_to_all x1, starting transfers between devices, on_device(): lax.all_to_all(rot_k, 'seq', split_axis=1, concat_axis=0, tiled=True)  3.49 us
  transfers between devices with their start and end apart: 5, of which 3 were waited for; matrix products, arithmetic and copies ran while one was open for 22% of the time, Pallas kernels for 0%

commit v1 on v0

v1 whole, which is shorter than its diff:
```python
import functools
import math

import jax
import jax.numpy as jnp
from jax import lax
from jax.experimental import pallas as pl
from jax.experimental.pallas import tpu as pltpu
from jax.sharding import PartitionSpec as P

HEAD_DIM = 128
STEPS = 20
PAIR = 2 * HEAD_DIM

masked_score = -1e30
norm_eps = 1e-06
shift_factor = 5.0
MESH = pl.DeviceIdType.MESH


def noise_level(step_value):
    progress = 1.0 - step_value / STEPS
    return shift_factor * progress / (1.0 + (shift_factor - 1.0) * progress)


def fill_tables(cos_ref, sin_ref, start, rows, first_token, dims):
    height, width = dims
    sixth = HEAD_DIM // 6
    time_pairs = (HEAD_DIM - 4 * sixth) // 2
    lane = lax.broadcasted_iota(jnp.int32, (8, HEAD_DIM), 1)
    pair = lane // 2
    is_time = pair < time_pairs
    is_row = pair < time_pairs + sixth
    pair_f = pair.astype(jnp.float32)
    space = pair_f - time_pairs
    exponent = jnp.where(
        is_time, pair_f / time_pairs, jnp.where(is_row, space / sixth, (space - sixth) / sixth)
    )
    freq = jnp.exp(exponent * -math.log(10000.0))[0:1]
    sign = jnp.where(lane % 2 == 0, -1.0, 1.0).astype(jnp.float32)[0:1]
    lanes = lax.broadcasted_iota(jnp.int32, (rows, HEAD_DIM), 1) // 2
    token = (first_token + lax.broadcasted_iota(jnp.int32, (rows, HEAD_DIM), 0)).astype(jnp.float32)
    h_vec = jnp.full((rows, HEAD_DIM), height.astype(jnp.float32))
    w_vec = jnp.full((rows, HEAD_DIM), width.astype(jnp.float32))
    frame = jnp.floor((token + 0.5) / (h_vec * w_vec))
    line = jnp.floor((token + 0.5) / w_vec)
    row = line - h_vec * jnp.floor((line + 0.5) / h_vec)
    col = token - w_vec * line
    position = jnp.where(lanes < time_pairs, frame, jnp.where(lanes < time_pairs + sixth, row, col))
    angles = position * freq
    cos_ref[start : start + rows, :] = jnp.cos(angles)
    sin_ref[start : start + rows, :] = jnp.sin(angles) * sign


def rotate(x, cos, sin, is_even):
    source = x.astype(jnp.float32)
    partner = jnp.where(
        is_even, pltpu.roll(source, HEAD_DIM - 1, 1), pltpu.roll(source, 1, 1)
    )
    return (source * cos + partner * sin).astype(jnp.bfloat16)


def kernel(
    n_seq,
    n_req,
    q_hbm,
    k_hbm,
    v_hbm,
    hidden_hbm,
    w_hbm,
    head_w,
    bias_ref,
    gate_ref,
    mod_ref,
    grid_ref,
    step_ref,
    guide_ref,
    latent_ref,
    next_ref,
    vel_ref,
    q_buf,
    k_buf,
    v_buf,
    hid_buf,
    w_buf,
    att_buf,
    cos_buf,
    sin_buf,
    pred_buf,
    other_buf,
    proj_buf,
    load_sem,
    kv_send,
    kv_recv,
    line_send,
    line_recv,
    x_send,
    x_recv,
    c_send,
    c_recv,
    p_send,
    p_recv,
):
    rows = q_buf.shape[0]
    width = q_buf.shape[1]
    pairs = width // PAIR
    shard = w_hbm.shape[0]
    half = shard // 2
    line_len = n_req // 2
    me_s = lax.axis_index("seq")
    me_c = lax.axis_index("cfg")
    me_r = lax.axis_index("req")
    place = me_r // 2
    x_mate = me_r + 1 - 2 * (me_r % 2)
    other = 1 - me_c

    def remote(src, dst, s_sem, r_sem, **target):
        return pltpu.make_async_remote_copy(
            src_ref=src, dst_ref=dst, send_sem=s_sem, recv_sem=r_sem,
            device_id=target, device_id_type=MESH,
        )

    barrier = pltpu.get_barrier_semaphore()
    for d in range(1, n_seq):
        pl.semaphore_signal(
            barrier, inc=1, device_id={"seq": lax.rem(me_s + d, n_seq)}, device_id_type=MESH
        )
    pl.semaphore_signal(barrier, inc=1, device_id={"cfg": other}, device_id_type=MESH)
    pl.semaphore_signal(barrier, inc=1, device_id={"req": x_mate}, device_id_type=MESH)
    for step in (2, n_req - 2):
        pl.semaphore_signal(
            barrier, inc=1, device_id={"req": lax.rem(me_r + step, n_req)}, device_id_type=MESH
        )

    loads = [
        pltpu.make_async_copy(q_hbm, q_buf, load_sem.at[0]),
        pltpu.make_async_copy(k_hbm, k_buf.at[0:rows, :], load_sem.at[1]),
        pltpu.make_async_copy(v_hbm, v_buf.at[0:rows, :], load_sem.at[2]),
        pltpu.make_async_copy(
            w_hbm, w_buf.at[pl.ds(pl.multiple_of(me_r * shard, shard), shard), :], load_sem.at[3]
        ),
        pltpu.make_async_copy(hidden_hbm, hid_buf, load_sem.at[4]),
    ]
    for load in loads:
        load.start()
    pl.semaphore_wait(barrier, n_seq + 3)

    def kv_copy(d, p, kind):
        cols = slice(p * PAIR, (p + 1) * PAIR)
        src = (k_hbm, v_hbm)[kind].at[:, cols]
        dst = (k_buf, v_buf)[kind].at[d * rows : (d + 1) * rows, cols]
        return remote(
            src, dst, kv_send.at[d - 1, p, kind], kv_recv.at[d - 1, p, kind],
            seq=lax.rem(me_s + d, n_seq),
        )

    kv = {}
    for p in range(pairs):
        for kind in range(2):
            for d in range(1, n_seq):
                kv[d, p, kind] = kv_copy(d, p, kind)

    def piece(owner, which):
        start = pl.multiple_of(owner * shard + which * half, half)
        return w_buf.at[pl.ds(start, half), :]

    own_src = w_hbm.at[pl.ds(pl.multiple_of(me_c * half, half), half), :]

    def toward(side):
        return jnp.maximum(me_r - 2, 0) if side == 0 else jnp.minimum(me_r + 2, n_req - 1)

    def can_pass(side):
        return place >= 1 if side == 0 else place <= line_len - 2

    def comes(side, k):
        return place + k <= line_len - 1 if side == 0 else place - k >= 0

    def owner_of(base, side, k):
        return base + 2 * k if side == 0 else base - 2 * k

    def line_copy(src, owner, side, k):
        return remote(
            src, piece(owner, me_c), line_send.at[side, k], line_recv.at[side, k], req=toward(side)
        )

    def x_copy(src, owner, side, k):
        return remote(src, piece(owner, me_c), x_send.at[side, k], x_recv.at[side, k], req=x_mate)

    def c_copy(owner, which, way, side, k):
        return remote(
            piece(owner, which), piece(owner, which),
            c_send.at[way, side, k], c_recv.at[way, side, k], cfg=other,
        )

    own_x = x_copy(own_src, me_r, 0, 0)
    own_line = [line_copy(own_src, me_r, side, 0) for side in range(2)]
    for d in range(1, n_seq):
        kv[d, 0, 0].start()
        kv[d, 0, 1].start()
    for side in range(2):
        @pl.when(can_pass(side))
        def _():
            own_line[side].start()
    own_x.start()
    for p in range(1, pairs):
        for d in range(1, n_seq):
            kv[d, p, 0].start()
            kv[d, p, 1].start()

    def line_step(k):
        for side in range(2):
            @pl.when(comes(side, k))
            def _():
                owner = owner_of(me_r, side, k)
                line_copy(piece(owner, me_c), owner, side, k - 1).wait_recv()
                if k < line_len - 1:
                    @pl.when(can_pass(side))
                    def _():
                        line_copy(piece(owner, me_c), owner, side, k).start()
                x_copy(piece(owner, me_c), owner, side, k).start()
                c_copy(owner, me_c, 0, side, k).start()

    def x_step(k):
        if k == 0:
            x_copy(own_src, x_mate, 0, 0).wait_recv()
            c_copy(x_mate, me_c, 1, 0, 0).start()
            return
        for side in range(2):
            @pl.when(comes(side, k))
            def _():
                owner = owner_of(x_mate, side, k)
                x_copy(piece(owner, me_c), owner, side, k).wait_recv()
                c_copy(owner, me_c, 1, side, k).start()

    def finish_gather():
        c_copy(x_mate, other, 1, 0, 0).wait_recv()
        for k in range(1, line_len):
            for side in range(2):
                @pl.when(comes(side, k))
                def _():
                    c_copy(owner_of(me_r, side, k), other, 0, side, k).wait_recv()
                    c_copy(owner_of(x_mate, side, k), other, 1, side, k).wait_recv()

    frames, height, across = grid_ref[0, 0], grid_ref[0, 1], grid_ref[0, 2]
    length = frames * height * across
    for d in range(n_seq):
        source = lax.rem(me_s + n_seq - d, n_seq)
        fill_tables(cos_buf, sin_buf, d * rows, rows, source * rows, (height, across))
    total = n_seq * rows
    is_even = lax.broadcasted_iota(jnp.int32, (1, HEAD_DIM), 1) % 2 == 0
    key_slot = lax.broadcasted_iota(jnp.int32, (1, total), 1)
    slot = key_slot // rows
    source = lax.rem(me_s + n_seq - slot, n_seq)
    live_keys = source * rows + key_slot % rows < length
    factor = math.log2(math.e) / math.sqrt(HEAD_DIM)

    loads[0].wait()
    loads[1].wait()
    loads[2].wait()

    def attend_pair(p):
        for d in range(1, n_seq):
            kv[d, p, 0].wait_recv()
            kv[d, p, 1].wait_recv()
        for h in (2 * p, 2 * p + 1):
            cols = slice(h * HEAD_DIM, (h + 1) * HEAD_DIM)
            rot_q = rotate(q_buf[:, cols], cos_buf[0:rows, :], sin_buf[0:rows, :], is_even)
            rot_k = rotate(k_buf[:, cols], cos_buf[...], sin_buf[...], is_even)
            scores = lax.dot_general(
                rot_q, rot_k, (((1,), (1,)), ((), ())), preferred_element_type=jnp.float32
            )
            scores = jnp.where(live_keys, scores, masked_score)
            top = jnp.max(scores, axis=-1, keepdims=True)
            weights = jnp.exp2((scores - top) * factor)
            weight_sum = jnp.sum(weights, axis=-1, keepdims=True)
            mixed = jnp.dot(
                weights.astype(jnp.bfloat16), v_buf[:, cols], preferred_element_type=jnp.float32
            )
            att_buf[:, cols] = (mixed / weight_sum).astype(jnp.bfloat16)

    spread = max(1, -(-(line_len - 1) // max(1, pairs - 1)))
    k = 1
    for p in range(pairs):
        if p < pairs - 1:
            for _ in range(spread):
                if k < line_len:
                    line_step(k)
                    x_step(k - 1)
                    k += 1
        if p == pairs - 1:
            x_step(line_len - 1)
            loads[3].wait()
            loads[4].wait()
            finish_gather()
            done = (pairs - 1) * PAIR
            proj_buf[...] = jnp.dot(
                att_buf[:, 0:done], w_buf[0:done, :], preferred_element_type=jnp.float32
            )
        attend_pair(p)

    last = (pairs - 1) * PAIR
    proj = proj_buf[...] + jnp.dot(
        att_buf[:, last:], w_buf[last:, :], preferred_element_type=jnp.float32
    )
    mixed = hid_buf[...].astype(jnp.float32) + gate_ref[...] * proj
    average = jnp.mean(mixed, axis=-1, keepdims=True)
    centered = mixed - average
    spread_sq = jnp.mean(centered * centered, axis=-1, keepdims=True)
    normed = centered * lax.rsqrt(spread_sq + norm_eps)
    modded = (normed * (1.0 + mod_ref[1:2, :]) + mod_ref[0:1, :]).astype(jnp.bfloat16)
    channels = head_w.shape[0]
    on_diag = lax.broadcasted_iota(jnp.int32, (channels, channels), 0) == lax.broadcasted_iota(
        jnp.int32, (channels, channels), 1
    )
    bias = jnp.sum(jnp.where(on_diag, bias_ref[...], 0.0), axis=1, keepdims=True)
    pred_buf[...] = (
        lax.dot_general(
            head_w[...], modded, (((1,), (1,)), ((), ())), preferred_element_type=jnp.float32
        )
        + bias
    )

    own_width = channels // 2
    swap = remote(
        pred_buf.at[pl.ds(pl.multiple_of(other * own_width, own_width), own_width), :],
        other_buf, p_send, p_recv, cfg=other,
    )
    swap.start()
    own_cols = pred_buf[pl.ds(pl.multiple_of(me_c * own_width, own_width), own_width), :]
    step_vec = jnp.full((own_width, rows), step_ref[0].astype(jnp.float32))
    delta = noise_level(step_vec + 1.0) - noise_level(step_vec)
    live = me_s * rows + lax.broadcasted_iota(jnp.int32, (own_width, rows), 1) < length
    guide = guide_ref[0]

    for copy in kv.values():
        copy.wait_send()
    own_x.wait_send()
    for side in range(2):
        @pl.when(can_pass(side))
        def _():
            own_line[side].wait_send()
    c_copy(x_mate, me_c, 1, 0, 0).wait_send()
    for k in range(1, line_len):
        for side in range(2):
            @pl.when(comes(side, k))
            def _():
                owner = owner_of(me_r, side, k)
                if k < line_len - 1:
                    @pl.when(can_pass(side))
                    def _():
                        line_copy(piece(owner, me_c), owner, side, k).wait_send()
                x_copy(piece(owner, me_c), owner, side, k).wait_send()
                c_copy(owner, me_c, 0, side, k).wait_send()
                c_copy(owner_of(x_mate, side, k), me_c, 1, side, k).wait_send()

    swap.wait()
    other_cols = other_buf[...]
    is_cond = me_c == 0
    cond = jnp.where(is_cond, own_cols, other_cols)
    uncond = jnp.where(is_cond, other_cols, own_cols)
    guided = uncond + guide * (cond - uncond)
    velocity = jnp.where(live, guided, 0.0)
    vel_ref[...] = velocity
    next_ref[...] = latent_ref[...] + delta * velocity


def solution(mesh):
    n_seq, n_req = mesh.shape["seq"], mesh.shape["req"]

    def on_device(
        queries,
        key_vectors,
        values,
        hidden,
        out_proj,
        head_weight,
        head_bias,
        attn_gate,
        shift_scale,
        grid_shape,
        step_index,
        guide_scale,
        latent,
    ):
        rows, width = queries.shape[2:]
        model = hidden.shape[3]
        channels = head_weight.shape[1]
        own_width = latent.shape[2]
        pairs = width // PAIR
        line_len = n_req // 2
        total = n_seq * rows
        any_spec = pl.BlockSpec(memory_space=pl.ANY)
        vmem = pl.BlockSpec(memory_space=pltpu.VMEM)
        smem = pl.BlockSpec(memory_space=pltpu.SMEM)
        dma = pltpu.SemaphoreType.DMA
        out = jax.ShapeDtypeStruct((own_width, rows), jnp.float32)
        next_t, vel_t = pl.pallas_call(
            functools.partial(kernel, n_seq, n_req),
            out_shape=(out, out),
            in_specs=[any_spec] * 5 + [vmem] * 4 + [smem] * 3 + [vmem],
            out_specs=(vmem, vmem),
            scratch_shapes=[
                pltpu.VMEM((rows, width), jnp.bfloat16),
                pltpu.VMEM((total, width), jnp.bfloat16),
                pltpu.VMEM((total, width), jnp.bfloat16),
                pltpu.VMEM((rows, model), jnp.bfloat16),
                pltpu.VMEM((width, model), jnp.bfloat16),
                pltpu.VMEM((rows, width), jnp.bfloat16),
                pltpu.VMEM((total, HEAD_DIM), jnp.float32),
                pltpu.VMEM((total, HEAD_DIM), jnp.float32),
                pltpu.VMEM((channels, rows), jnp.float32),
                pltpu.VMEM((own_width, rows), jnp.float32),
                pltpu.VMEM((rows, model), jnp.float32),
                dma((5,)),
                dma((n_seq - 1, pairs, 2)),
                dma((n_seq - 1, pairs, 2)),
                dma((2, line_len)),
                dma((2, line_len)),
                dma((2, line_len)),
                dma((2, line_len)),
                dma((2, 2, line_len)),
                dma((2, 2, line_len)),
                dma(()),
                dma(()),
            ],
            compiler_params=pltpu.CompilerParams(
                collective_id=0, has_side_effects=True, vmem_limit_bytes=56 * 1024 * 1024
            ),
        )(
            queries[0, 0],
            key_vectors[0, 0],
            values[0, 0],
            hidden[0, 0],
            out_proj,
            head_weight.T,
            head_bias[None, :],
            attn_gate,
            shift_scale[0],
            grid_shape,
            step_index,
            guide_scale,
            latent[0].T,
        )
        return (next_t.T[None], vel_t.T[None])

    return jax.shard_map(
        on_device,
        mesh=mesh,
        in_specs=(
            P("req", "cfg", "seq", None),
            P("req", "cfg", "seq", None),
            P("req", "cfg", "seq", None),
            P("req", "cfg", "seq", None),
            P("req", None),
            P(),
            P(),
            P("req", None),
            P("req", None, None),
            P("req", None),
            P("req"),
            P("req"),
            P("req", "seq", "cfg"),
        ),
        out_specs=(P("req", "seq", "cfg"), P("req", "seq", "cfg")),
        check_vma=False,
    )
```

time: 88.6 us -> 39.2 us (0.44)
  Pallas kernels: 0 us -> 35.1 us
  between operations: 22.4 us -> 1.94 us
  waiting for transfers between devices: 17.3 us -> 0 us
  blocking collectives: 12 us -> 0 us
  starting transfers between devices: 10.6 us -> 0 us
  other arithmetic: 10.1 us -> 0 us
  local copies, waits for them, and re-layouts: 10.5 us -> 2 us
  matrix products: 5.09 us -> 0 us
    pallas_call x0 -> x1, Pallas kernels: none -> 35.1 us  [on_device(): pl.pallas_call(functools.partial(kernel, n_seq, n_req), out_shape=(out, o...]
    all_to_all x3 -> x0, waiting for transfers between devices: 16.6 us -> none  [the longest x1 6.46 us: on_device(): lax.all_to_all(head_result, 'seq', split_axis=0, concat_axis=1, tiled=True)]
    all_to_all x1 -> x0, blocking collectives: 12 us -> none  [on_device(): lax.all_to_all(rot_q, 'seq', split_axis=1, concat_axis=0, tiled=True)]
    all_to_all x3 -> x0, starting transfers between devices: 10.5 us -> none  [the longest x1 3.49 us: on_device(): lax.all_to_all(values[0, 0], 'seq', split_axis=1, concat_axis=0, tiled=True)]
    convert_element_type x3 -> x0, other arithmetic: 5.66 us -> none  [the longest x1 5.45 us: rotary(): return turned.astype(jnp.bfloat16)]
    dot_general x4 -> x0, matrix products: 5.09 us -> none  [the longest x1 2.98 us: on_device(): jnp.dot(attended, lax.all_gather(out_proj, 'req', axis=0, tiled=True), pr...]
    convert_element_type x3 -> x0, local copies, waits for them, and re-layouts: 4.55 us -> none  [the longest x2 4.14 us: rotary(): source = vectors.astype(jnp.float32)]
    all_to_all x4 -> x0, local copies, waits for them, and re-layouts: 2.46 us -> none  [the longest x2 1.24 us: on_device(): lax.all_to_all(values[0, 0], 'seq', split_axis=1, concat_axis=0, tiled=True)]
  transfers between devices with their start and end apart: 5 -> 0, of which waited for: 3 -> 0; matrix products, arithmetic and copies ran while one was open for 22% -> 0% of each run, Pallas kernels for 0% -> 0%
where the time goes in v1:
time: 39.2 us; the launch traced here: 39 us
  Pallas kernels  35.1 us (90%)
  local copies, waits for them, and re-layouts  2 us (5%)
  between operations  1.94 us (5%)
    pallas_call x1, Pallas kernels, on_device(): pl.pallas_call(functools.partial(kernel, n_seq, n_req), out_shape=(out, o...  35.1 us
    unnamed x4, local copies, waits for them, and re-layouts  2 us

profile of v1, /device:TPU:0, one launch (start us, length us, event | category | flops | bytes accessed | tf_op | source)
XLA Modules:
  0.0 39.0 jit_solution(9802037549178570140)
XLA Ops:
  1.9 35.1 %shard_map.140 = (f32[32,256]{1,0:T(8,128)}, f32[32,256]{1,0:T(8,128)}) custom-call(bf16[256,1024]{1,0:T(8,128)(2,1)} %bitcast.17, bf16[256,1024]{1,0:T(8,128)(2,1)} %bitcast.18, bf16[256,1024]{1,0:T(8,128)(2,1)} %bitcast.19, bf16[256,1536]{1,0:T(8,128)(2,1)} %bitcast.16, bf16[128,1536]{1,0:T(8,128)(2,1)} %w_hbm.1, bf16[64,1536]{1,0:T(8,128)(2,1)} %bitcast.20, ...), custom_call_target="tpu_custom_call" | custom-call | tf_op jit(solution)/shard_map/pallas_call | solution.py:397
  37.0 0.0 copy-start
  37.0 1.4 %copy.19 = f32[1,256,32]{1,2,0:T(8,128)} copy(f32[1,256,32]{1,2,0:T(8,128)} %bitcast.23) | data formatting | bytes 65536
  38.4 0.0 copy-done
  38.4 0.6 %copy.20 = f32[1,256,32]{1,2,0:T(8,128)} copy(f32[1,256,32]{1,2,0:T(8,128)S(1)} %bitcast.22) | data formatting | bytes 65536
Async XLA Ops:
  37.0 1.4 %copy-start = (f32[32,256]{1,0:T(8,128)S(1)}, f32[32,256]{1,0:T(8,128)}, u32[]{:S(2)}) copy-start(f32[32,256]{1,0:T(8,128)} %get-tuple-element.5) | copy-start | bytes 98308

commit v2 on v1

--- a/solution.py
+++ b/solution.py
@@ -68,16 +68,14 @@
     v_hbm,
     hidden_hbm,
     w_hbm,
-    head_w,
-    bias_ref,
-    gate_ref,
-    mod_ref,
-    grid_ref,
-    step_ref,
-    guide_ref,
-    latent_ref,
-    next_ref,
-    vel_ref,
+    head_w_hbm,
+    bias_hbm,
+    gate_hbm,
+    mod_hbm,
+    grid_hbm,
+    step_hbm,
+    guide_hbm,
+    out_ref,
     q_buf,
     k_buf,
     v_buf,
@@ -89,6 +87,13 @@
     pred_buf,
     other_buf,
     proj_buf,
+    head_w,
+    bias_ref,
+    gate_ref,
+    mod_ref,
+    grid_ref,
+    step_ref,
+    guide_ref,
     load_sem,
     kv_send,
     kv_recv,
@@ -140,6 +145,13 @@
             w_hbm, w_buf.at[pl.ds(pl.multiple_of(me_r * shard, shard), shard), :], load_sem.at[3]
         ),
         pltpu.make_async_copy(hidden_hbm, hid_buf, load_sem.at[4]),
+        pltpu.make_async_copy(grid_hbm, grid_ref, load_sem.at[5]),
+        pltpu.make_async_copy(step_hbm, step_ref, load_sem.at[6]),
+        pltpu.make_async_copy(guide_hbm, guide_ref, load_sem.at[7]),
+        pltpu.make_async_copy(head_w_hbm, head_w, load_sem.at[8]),
+        pltpu.make_async_copy(bias_hbm, bias_ref, load_sem.at[9]),
+        pltpu.make_async_copy(gate_hbm, gate_ref, load_sem.at[10]),
+        pltpu.make_async_copy(mod_hbm, mod_ref, load_sem.at[11]),
     ]
     for load in loads:
         load.start()
@@ -241,6 +253,7 @@
                     c_copy(owner_of(me_r, side, k), other, 0, side, k).wait_recv()
                     c_copy(owner_of(x_mate, side, k), other, 1, side, k).wait_recv()
 
+    loads[5].wait()
     frames, height, across = grid_ref[0, 0], grid_ref[0, 1], grid_ref[0, 2]
     length = frames * height * across
     for d in range(n_seq):
@@ -259,11 +272,11 @@
     loads[2].wait()
 
     def attend_pair(p):
+        heads = [slice(h * HEAD_DIM, (h + 1) * HEAD_DIM) for h in (2 * p, 2 * p + 1)]
         for d in range(1, n_seq):
             kv[d, p, 0].wait_recv()
-            kv[d, p, 1].wait_recv()
-        for h in (2 * p, 2 * p + 1):
-            cols = slice(h * HEAD_DIM, (h + 1) * HEAD_DIM)
+        staged = []
+        for cols in heads:
             rot_q = rotate(q_buf[:, cols], cos_buf[0:rows, :], sin_buf[0:rows, :], is_even)
             rot_k = rotate(k_buf[:, cols], cos_buf[...], sin_buf[...], is_even)
             scores = lax.dot_general(
@@ -273,9 +286,11 @@
             top = jnp.max(scores, axis=-1, keepdims=True)
             weights = jnp.exp2((scores - top) * factor)
             weight_sum = jnp.sum(weights, axis=-1, keepdims=True)
-            mixed = jnp.dot(
-                weights.astype(jnp.bfloat16), v_buf[:, cols], preferred_element_type=jnp.float32
-            )
+            staged.append((weights.astype(jnp.bfloat16), weight_sum))
+        for d in range(1, n_seq):
+            kv[d, p, 1].wait_recv()
+        for cols, (weights, weight_sum) in zip(heads, staged):
+            mixed = jnp.dot(weights, v_buf[:, cols], preferred_element_type=jnp.float32)
             att_buf[:, cols] = (mixed / weight_sum).astype(jnp.bfloat16)
 
     spread = max(1, -(-(line_len - 1) // max(1, pairs - 1)))
@@ -291,6 +306,8 @@
             x_step(line_len - 1)
             loads[3].wait()
             loads[4].wait()
+            for load in loads[6:]:
+                load.wait()
             finish_gather()
             done = (pairs - 1) * PAIR
             proj_buf[...] = jnp.dot(
@@ -360,8 +377,8 @@
     uncond = jnp.where(is_cond, other_cols, own_cols)
     guided = uncond + guide * (cond - uncond)
     velocity = jnp.where(live, guided, 0.0)
-    vel_ref[...] = velocity
-    next_ref[...] = latent_ref[...] + delta * velocity
+    out_ref[0:own_width, :] = velocity
+    out_ref[own_width:, :] = delta * velocity
 
 
 def solution(mesh):
@@ -390,15 +407,12 @@
         line_len = n_req // 2
         total = n_seq * rows
         any_spec = pl.BlockSpec(memory_space=pl.ANY)
-        vmem = pl.BlockSpec(memory_space=pltpu.VMEM)
-        smem = pl.BlockSpec(memory_space=pltpu.SMEM)
         dma = pltpu.SemaphoreType.DMA
-        out = jax.ShapeDtypeStruct((own_width, rows), jnp.float32)
-        next_t, vel_t = pl.pallas_call(
+        out = pl.pallas_call(
             functools.partial(kernel, n_seq, n_req),
-            out_shape=(out, out),
-            in_specs=[any_spec] * 5 + [vmem] * 4 + [smem] * 3 + [vmem],
-            out_specs=(vmem, vmem),
+            out_shape=jax.ShapeDtypeStruct((2 * own_width, rows), jnp.float32),
+            in_specs=[any_spec] * 12,
+            out_specs=pl.BlockSpec(memory_space=pltpu.VMEM),
             scratch_shapes=[
                 pltpu.VMEM((rows, width), jnp.bfloat16),
                 pltpu.VMEM((total, width), jnp.bfloat16),
@@ -411,7 +425,14 @@
                 pltpu.VMEM((channels, rows), jnp.float32),
                 pltpu.VMEM((own_width, rows), jnp.float32),
                 pltpu.VMEM((rows, model), jnp.float32),
-                dma((5,)),
+                pltpu.VMEM((channels, model), jnp.bfloat16),
+                pltpu.VMEM((1, channels), jnp.float32),
+                pltpu.VMEM((1, model), jnp.float32),
+                pltpu.VMEM((2, model), jnp.float32),
+                pltpu.SMEM((1, 3), jnp.int32),
+                pltpu.SMEM((1,), jnp.int32),
+                pltpu.SMEM((1,), jnp.float32),
+                dma((12,)),
                 dma((n_seq - 1, pairs, 2)),
                 dma((n_seq - 1, pairs, 2)),
                 dma((2, line_len)),
@@ -439,9 +460,9 @@
             grid_shape,
             step_index,
             guide_scale,
-            latent[0].T,
-        )
-        return (next_t.T[None], vel_t.T[None])
+        )
+        velocity = out[0:own_width].T[None]
+        return (latent + out[own_width:].T[None], velocity)
 
     return jax.shard_map(
         on_device,

time: 39.2 us -> 37.7 us (0.962)
  Pallas kernels: 35.1 us -> 33.5 us
  other arithmetic: 0 us -> 0.62 us
  local copies, waits for them, and re-layouts: 2 us -> 1.45 us
    unnamed x4, local copies, waits for them, and re-layouts: 2 us -> 0.01 us
    pallas_call x1, Pallas kernels: 35.1 us -> 33.5 us  [on_device(): pl.pallas_call(functools.partial(kernel, n_seq, n_req), out_shape=jax.Sha...]
    broadcast_in_dim x0 -> x1, local copies, waits for them, and re-layouts: none -> 1.44 us  [on_device(): velocity = out[0:own_width].T[None]]
    add x0 -> x1, other arithmetic: none -> 0.62 us  [on_device(): return (latent + out[own_width:].T[None], velocity)]
where the time goes in v2:
time: 37.7 us; the launch traced here: 37.5 us
  Pallas kernels  33.5 us (89%)
  between operations  1.95 us (5%)
  local copies, waits for them, and re-layouts  1.45 us (4%)
  other arithmetic  0.62 us (2%)
    pallas_call x1, Pallas kernels, on_device(): pl.pallas_call(functools.partial(kernel, n_seq, n_req), out_shape=jax.Sha...  33.5 us
    broadcast_in_dim x1, local copies, waits for them, and re-layouts, on_device(): velocity = out[0:own_width].T[None]  1.44 us

profile of v2, /device:TPU:0, one launch (start us, length us, event | category | flops | bytes accessed | tf_op | source)
XLA Modules:
  0.0 37.5 jit_solution(1984999652164241871)
XLA Ops:
  1.9 0.0 copy-start.1
  1.9 33.5 %shard_map.140 = f32[64,256]{1,0:T(8,128)} custom-call(bf16[256,1024]{1,0:T(8,128)(2,1)} %bitcast.16, bf16[256,1024]{1,0:T(8,128)(2,1)} %bitcast.17, bf16[256,1024]{1,0:T(8,128)(2,1)} %bitcast.18, bf16[256,1536]{1,0:T(8,128)(2,1)} %bitcast.15, bf16[128,1536]{1,0:T(8,128)(2,1)} %w_hbm.1, bf16[64,1536]{1,0:T(8,128)(2,1)} %bitcast.19, f32[1,64]{1,0:T(1,128)} %bitcast.21, ...), custom_call_target="tpu_custom_call" | custom-call | tf_op jit(solution)/shard_map/pallas_call | solution.py:411
  35.5 0.0 copy-start
  35.5 1.4 %slice_bitcast_fusion = f32[1,256,32]{1,2,0:T(8,128)} fusion(f32[64,256]{1,0:T(8,128)} %shard_map.140), kind=kLoop, calls=%fused_computation.1 | loop fusion | bytes 65536 | tf_op jit(solution)/shard_map/broadcast_in_dim | solution.py:464
  36.9 0.0 copy-done.1
  36.9 0.0 copy-done
  36.9 0.6 %bitcast_add_fusion = f32[1,256,32]{1,2,0:T(8,128)} fusion(f32[1,256,32]{1,2,0:T(8,128)S(1)} %copy-done.1, f32[64,256]{1,0:T(8,128)S(1)} %copy-done), kind=kLoop, calls=%fused_computation | loop fusion | flops 8192 | bytes 98304 | tf_op jit(solution)/shard_map/add | solution.py:465
Async XLA Ops:
  1.9 35.0 %copy-start.1 = (f32[1,256,32]{1,2,0:T(8,128)S(1)}, f32[1,256,32]{1,2,0:T(8,128)}, u32[]{:S(2)}) copy-start(f32[1,256,32]{1,2,0:T(8,128)} %param.25) | copy-start | bytes 98308
  35.5 1.5 %copy-start = (f32[64,256]{1,0:T(8,128)S(1)}, f32[64,256]{1,0:T(8,128)}, u32[]{:S(2)}) copy-start(f32[64,256]{1,0:T(8,128)} %shard_map.140) | copy-start | bytes 196612

commit v3 on v2

--- a/solution.py
+++ b/solution.py
@@ -153,13 +153,15 @@
         pltpu.make_async_copy(gate_hbm, gate_ref, load_sem.at[10]),
         pltpu.make_async_copy(mod_hbm, mod_ref, load_sem.at[11]),
     ]
-    for load in loads:
-        load.start()
+    for i in (1, 2, 0, *range(3, len(loads))):
+        loads[i].start()
+    loads[1].wait()
+    loads[2].wait()
     pl.semaphore_wait(barrier, n_seq + 3)
 
     def kv_copy(d, p, kind):
         cols = slice(p * PAIR, (p + 1) * PAIR)
-        src = (k_hbm, v_hbm)[kind].at[:, cols]
+        src = (k_buf, v_buf)[kind].at[0:rows, cols]
         dst = (k_buf, v_buf)[kind].at[d * rows : (d + 1) * rows, cols]
         return remote(
             src, dst, kv_send.at[d - 1, p, kind], kv_recv.at[d - 1, p, kind],
@@ -268,8 +270,6 @@
     factor = math.log2(math.e) / math.sqrt(HEAD_DIM)
 
     loads[0].wait()
-    loads[1].wait()
-    loads[2].wait()
 
     def attend_pair(p):
         heads = [slice(h * HEAD_DIM, (h + 1) * HEAD_DIM) for h in (2 * p, 2 * p + 1)]
@@ -310,16 +310,15 @@
                 load.wait()
             finish_gather()
             done = (pairs - 1) * PAIR
-            proj_buf[...] = jnp.dot(
+            proj_buf[...] = hid_buf[...].astype(jnp.float32) + gate_ref[...] * jnp.dot(
                 att_buf[:, 0:done], w_buf[0:done, :], preferred_element_type=jnp.float32
             )
         attend_pair(p)
 
     last = (pairs - 1) * PAIR
-    proj = proj_buf[...] + jnp.dot(
+    mixed = proj_buf[...] + gate_ref[...] * jnp.dot(
         att_buf[:, last:], w_buf[last:, :], preferred_element_type=jnp.float32
     )
-    mixed = hid_buf[...].astype(jnp.float32) + gate_ref[...] * proj
     average = jnp.mean(mixed, axis=-1, keepdims=True)
     centered = mixed - average
     spread_sq = jnp.mean(centered * centered, axis=-1, keepdims=True)
@@ -344,7 +343,7 @@
     )
     swap.start()
     own_cols = pred_buf[pl.ds(pl.multiple_of(me_c * own_width, own_width), own_width), :]
-    step_vec = jnp.full((own_width, rows), step_ref[0].astype(jnp.float32))
+    step_vec = jnp.full((8, rows), step_ref[0].astype(jnp.float32))
     delta = noise_level(step_vec + 1.0) - noise_level(step_vec)
     live = me_s * rows + lax.broadcasted_iota(jnp.int32, (own_width, rows), 1) < length
     guide = guide_ref[0]
@@ -375,10 +374,9 @@
     is_cond = me_c == 0
     cond = jnp.where(is_cond, own_cols, other_cols)
     uncond = jnp.where(is_cond, other_cols, own_cols)
-    guided = uncond + guide * (cond - uncond)
-    velocity = jnp.where(live, guided, 0.0)
-    out_ref[0:own_width, :] = velocity
-    out_ref[own_width:, :] = delta * velocity
+    out_ref[0:own_width, :] = jnp.where(live, uncond, 0.0)
+    out_ref[own_width : 2 * own_width, :] = jnp.where(live, guide * (cond - uncond), 0.0)
+    out_ref[2 * own_width :, :] = delta
 
 
 def solution(mesh):
@@ -410,7 +408,7 @@
         dma = pltpu.SemaphoreType.DMA
         out = pl.pallas_call(
             functools.partial(kernel, n_seq, n_req),
-            out_shape=jax.ShapeDtypeStruct((2 * own_width, rows), jnp.float32),
+            out_shape=jax.ShapeDtypeStruct((2 * own_width + 8, rows), jnp.float32),
             in_specs=[any_spec] * 12,
             out_specs=pl.BlockSpec(memory_space=pltpu.VMEM),
             scratch_shapes=[
@@ -461,8 +459,9 @@
             step_index,
             guide_scale,
         )
-        velocity = out[0:own_width].T[None]
-        return (latent + out[own_width:].T[None], velocity)
+        velocity = out[0:own_width] + out[own_width : 2 * own_width]
+        next_latent = latent[0].T + out[2 * own_width : 2 * own_width + 1] * velocity
+        return (next_latent.T[None], velocity.T[None])
 
     return jax.shard_map(
         on_device,

time: 37.7 us -> 37.5 us (level)
  local copies, waits for them, and re-layouts: 1.45 us -> 0.65 us
  other arithmetic: 0.62 us -> 1.41 us
    broadcast_in_dim x1 -> x0, local copies, waits for them, and re-layouts: 1.44 us -> none  [on_device(): velocity = out[0:own_width].T[None]]
    broadcast_in_dim x0 -> x1, other arithmetic: none -> 1.41 us  [on_device(): return (next_latent.T[None], velocity.T[None])]
    slice x0 -> x2, local copies, waits for them, and re-layouts: none -> 0.64 us  [on_device(): next_latent = latent[0].T + out[2 * own_width:2 * own_width + 1] * velocity]
    add x1 -> x0, other arithmetic: 0.62 us -> none  [on_device(): return (latent + out[own_width:].T[None], velocity)]
where the time goes in v3:
time: 37.5 us; the launch traced here: 37.3 us
  Pallas kernels  33.3 us (89%)
  between operations  1.96 us (5%)
  other arithmetic  1.41 us (4%)
  local copies, waits for them, and re-layouts  0.65 us (2%)
    pallas_call x1, Pallas kernels, on_device(): pl.pallas_call(functools.partial(kernel, n_seq, n_req), out_shape=jax.Sha...  33.3 us
    broadcast_in_dim x1, other arithmetic, on_device(): return (next_latent.T[None], velocity.T[None])  1.41 us

profile of v3, /device:TPU:0, one launch (start us, length us, event | category | flops | bytes accessed | tf_op | source)
XLA Modules:
  0.0 37.3 jit_solution(9654829717123880379)
XLA Ops:
  1.9 0.0 copy-start
  1.9 33.3 %shard_map.140 = f32[72,256]{1,0:T(8,128)} custom-call(bf16[256,1024]{1,0:T(8,128)(2,1)} %bitcast.23, bf16[256,1024]{1,0:T(8,128)(2,1)} %bitcast.24, bf16[256,1024]{1,0:T(8,128)(2,1)} %bitcast.25, bf16[256,1536]{1,0:T(8,128)(2,1)} %bitcast.22, bf16[128,1536]{1,0:T(8,128)(2,1)} %w_hbm.1, bf16[64,1536]{1,0:T(8,128)(2,1)} %bitcast.27, f32[1,64]{1,0:T(1,128)} %bitcast.29, ...), custom_call_target="tpu_custom_call" | custom-call | tf_op jit(solution)/shard_map/pallas_call | solution.py:409
  35.2 0.0 slice-start
  35.2 0.0 copy-done
  35.2 0.6 %slice-done = f32[1,256]{1,0:T(1,128)S(1)} async-done(((f32[72,256]{1,0:T(8,128)}), f32[1,256]{1,0:T(1,128)S(1)}, s32[]{:S(2)}) %slice-start) | async-done | bytes 1048 | tf_op jit(solution)/shard_map/slice | solution.py:463
  35.9 1.4 %fusion.1 = (f32[1,256,32]{1,2,0:T(8,128)}, f32[1,256,32]{1,2,0:T(8,128)}) fusion(f32[72,256]{1,0:T(8,128)} %shard_map.140, f32[256]{0:T(256)S(1)} %bitcast.26, f32[1,256,32]{1,2,0:T(8,128)S(1)} %copy-done), kind=kLoop, calls=%fused_computation.3 | loop fusion | flops 24576 | bytes 164864 | tf_op jit(solution)/shard_map/broadcast_in_dim | solution.py:464
Async XLA Ops:
  1.9 33.3 %copy-start = (f32[1,256,32]{1,2,0:T(8,128)S(1)}, f32[1,256,32]{1,2,0:T(8,128)}, u32[]{:S(2)}) copy-start(f32[1,256,32]{1,2,0:T(8,128)} %param.25) | copy-start | bytes 98308
  35.2 0.7 %slice-start = ((f32[72,256]{1,0:T(8,128)}), f32[1,256]{1,0:T(1,128)S(1)}, s32[]{:S(2)}) async-start(f32[72,256]{1,0:T(8,128)} %shard_map.140), calls=%async_computation | async-start | bytes 2048 | tf_op jit(solution)/shard_map/slice | solution.py:463
